TPU v7x, 32 devices: a whole 2x2x4 slice. The times are simulated.
32 devices in a mesh: space: 16 (over z, x, core), ens: 2 (over y).
Axes of the slice: x: 2, y: 2, z: 4, core: 2. Of those that a mesh axis runs over, the one named last changes fastest.
Arguments:
- params: float32 [64, 256, 512], P('ens', 'space'), may hold values from 0.55 to 0.8
- base_thickness: float32 [256, 512], P('space'), may hold values from 0.5 to 3
- balance: float32 [256, 512], P('space'), may hold values from -0.1 to 0.3
- step_count: int32 [64], replicated, may hold values from 8 to 32, as said below
- obs_index: int32 [4096], P('space'), may hold values from 0 to 8191
- observed: float32 [4096], P('space'), may hold values from 0.5 to 2
- noise_var: float32 [4096], P('space'), may hold values from 0.5 to 4
Outputs:
- thickness: float32 [64, 256, 512], P('ens', 'space')
- updated: float32 [64, 256, 512], P('ens', 'space')
Inputs may be any that keep to these rules, and one draw needn't show every extreme that they name: `step_count`: some member runs exactly 32 steps.
All inputs are finite; a program needn't handle non-finite values.
Results may differ from a plain program's by a relative error of at most 0.000074.
Values sent between devices are 32-bit elements; how exact they have to be, the bound alone decides.
A program may use at most 64 MiB of HBM per device.

v0:
```python
import jax
import jax.numpy as jnp
from jax import lax
from jax.sharding import PartitionSpec as P

time_step = 0.11


def padded_2(block, sides, width):
    for axis, dim in sides:
        count = lax.axis_size(axis)
        forward = [(i, i + 1) for i in range(count - 1)]
        backward = [(target, source) for source, target in forward]
        low = lax.ppermute(
            lax.slice_in_dim(block, block.shape[dim] - width, None, axis=dim), axis, forward
        )
        high = lax.ppermute(lax.slice_in_dim(block, 0, width, axis=dim), axis, backward)
        block = jnp.concatenate([low, block, high], axis=dim)
    return block


def stencil(padded, slip_padded, thickness, balance):
    diffusivity = slip_padded * padded * padded / (1.0 + padded * padded)
    centre = diffusivity[:, 1:-1, 1:-1]
    divergence = jnp.zeros_like(thickness)
    for row_part, col_part in (
        (slice(2, None), slice(1, -1)),
        (slice(None, -2), slice(1, -1)),
        (slice(1, -1), slice(2, None)),
        (slice(1, -1), slice(None, -2)),
    ):
        divergence = divergence + 0.5 * (diffusivity[:, row_part, col_part] + centre) * (
            padded[:, row_part, col_part] - thickness
        )
    return thickness + time_step * (divergence + balance)


def ensemble_terms(predicted, observed, noise_var):
    members = predicted.shape[0]
    scaling = lax.rsqrt(noise_var)
    average = jnp.mean(predicted, axis=0)
    anomalies = (predicted - average) * scaling / jnp.sqrt(jnp.float32(members - 1))
    mismatch = (observed - predicted) * scaling
    gram = jnp.dot(anomalies, anomalies.T, precision=lax.Precision.HIGHEST)
    cross = jnp.dot(anomalies, mismatch.T, precision=lax.Precision.HIGHEST)
    return (gram, cross)


def solve_weights(gram, cross):
    members = gram.shape[0]
    factor = jnp.linalg.cholesky(gram + jnp.eye(members, dtype=gram.dtype))
    inner = lax.linalg.triangular_solve(factor, cross, left_side=True, lower=True)
    result = lax.linalg.triangular_solve(
        factor, inner, left_side=True, lower=True, transpose_a=True
    )
    return result / jnp.sqrt(jnp.float32(members - 1))


def shards(params, base_thickness, balance, step_count, obs_index, observed, noise_var):
    members_dev = params.shape[0]
    ens_index = lax.axis_index("ens")
    members = members_dev * lax.axis_size("ens")
    own_counts = lax.dynamic_slice_in_dim(step_count, ens_index * members_dev, members_dev)
    longest = jnp.max(own_counts)
    initial = jnp.broadcast_to(base_thickness[None], params.shape)
    slip_rows = padded_2(jnp.exp(params), (("space", 1),), 1)
    slip_padded = jnp.pad(slip_rows, ((0, 0), (0, 0), (1, 1)))

    def advance(step_index, thickness):
        rimmed = padded_2(thickness, (("space", 1),), 1)
        padded = jnp.pad(rimmed, ((0, 0), (0, 0), (1, 1)))
        moved = stencil(padded, slip_padded, thickness, balance)
        return jnp.where((step_index < own_counts)[:, None, None], moved, thickness)

    thickness = lax.fori_loop(0, longest, advance, initial)
    tile_cells = params.shape[1] * params.shape[2]
    predicted = jnp.take(thickness.reshape(members_dev, tile_cells), obs_index, axis=1)
    obs_block = lax.all_to_all(predicted, "ens", split_axis=1, concat_axis=0, tiled=True)
    block_width = obs_block.shape[1]
    observed_part = lax.dynamic_slice_in_dim(observed, ens_index * block_width, block_width)
    noise_part = lax.dynamic_slice_in_dim(noise_var, ens_index * block_width, block_width)
    gram, cross = ensemble_terms(obs_block, observed_part, noise_part)
    gram, cross = lax.psum((gram, cross), ("space", "ens"))
    weights = solve_weights(gram, cross)
    weight_cols = lax.dynamic_slice_in_dim(weights, ens_index * members_dev, members_dev, 1)
    piece = lax.all_gather(params, "ens", axis=0, tiled=True)
    piece_rows = piece.shape[0]
    flat_piece = piece.reshape(piece_rows, tile_cells)
    weighted = jnp.dot(weight_cols.T, flat_piece, precision=lax.Precision.HIGHEST)
    weighted, member_total = (weighted, jnp.sum(flat_piece, axis=0))
    column_sums = jnp.sum(weight_cols, axis=0)
    increment = weighted - column_sums[:, None] * member_total[None, :] / members
    updated = params + increment.reshape(params.shape)
    return (thickness, updated)


def solution(mesh):
    in_specs = (
        P("ens", "space", None),
        P("space", None),
        P("space", None),
        P(),
        P("space"),
        P("space"),
        P("space"),
    )
    out_specs = (P("ens", "space", None), P("ens", "space", None))
    return jax.shard_map(shards, mesh=mesh, in_specs=in_specs, out_specs=out_specs, check_vma=False)
```

profile of v0, /device:TPU:0, one launch (start us, length us, event | category | flops | bytes accessed | tf_op | source)
XLA Modules:
  0.0 560.8 jit_solution(4297953380214112374)
XLA Ops:
  19.3 447.2 %while.12 = (s32[]{:T(128)}, f32[32,16,512]{2,1,0:T(8,128)}, s32[]{:T(128)}, s32[32]{0:T(128)S(1)}, f32[32,18,514]{2,1,0:T(8,128)S(1)}, /*index=5*/f32[16,512]{1,0:T(8,128)S(1)}, s32[]{:T(128)}) while((s32[]{:T(128)}, f32[32,16,512]{2,1,0:T(8,128)}, s32[]{:T(128)}, s32[32]{0:T(128)S(1)}, f32[32,18,514]{2,1,0:T(8,128)S(1)}, ...), condition=%wide.region_2.3_spmd, body=%wide.region_1.2_spmd.sunk | while | flops 10402466 | bytes 17217376 | solution.py:75
  22.6 5.4 collective-permute-start.1
  49.1 6.0 %collective-permute-start.1 = (f32[32,1,512]{2,1,0:T(1,128)S(1)}, f32[32,1,512]{2,1,0:T(1,128)S(1)}, u32[]{:S(2)}, u32[]{:S(2)}) collective-permute-start(f32[32,1,512]{2,1,0:T(1,128)S(1)} %get-tuple-element.150), channel_id=1, source_target_pairs={{0,2},{2,4},{4,6},{6,8},{8,10},{10,12},{12,14},{14,16},{16,18},{18... | collective-permute-start | bytes 196616 | tf_op jit(solution)/shard_map/while/body/ppermute | solution.py:14
  63.0 5.4 collective-permute-start.1
  76.4 6.0 %collective-permute-start.1 = (f32[32,1,512]{2,1,0:T(1,128)S(1)}, f32[32,1,512]{2,1,0:T(1,128)S(1)}, u32[]{:S(2)}, u32[]{:S(2)}) collective-permute-start(f32[32,1,512]{2,1,0:T(1,128)S(1)} %get-tuple-element.150), channel_id=1, source_target_pairs={{0,2},{2,4},{4,6},{6,8},{8,10},{10,12},{12,14},{14,16},{16,18},{18... | collective-permute-start | bytes 196616 | tf_op jit(solution)/shard_map/while/body/ppermute | solution.py:14
  90.3 6.0 %collective-permute-start.1 = (f32[32,1,512]{2,1,0:T(1,128)S(1)}, f32[32,1,512]{2,1,0:T(1,128)S(1)}, u32[]{:S(2)}, u32[]{:S(2)}) collective-permute-start(f32[32,1,512]{2,1,0:T(1,128)S(1)} %get-tuple-element.150), channel_id=1, source_target_pairs={{0,2},{2,4},{4,6},{6,8},{8,10},{10,12},{12,14},{14,16},{16,18},{18... | collective-permute-start | bytes 196616 | tf_op jit(solution)/shard_map/while/body/ppermute | solution.py:14
  130.8 5.3 collective-permute-start.1
  144.0 6.2 %collective-permute-start.1 = (f32[32,1,512]{2,1,0:T(1,128)S(1)}, f32[32,1,512]{2,1,0:T(1,128)S(1)}, u32[]{:S(2)}, u32[]{:S(2)}) collective-permute-start(f32[32,1,512]{2,1,0:T(1,128)S(1)} %get-tuple-element.150), channel_id=1, source_target_pairs={{0,2},{2,4},{4,6},{6,8},{8,10},{10,12},{12,14},{14,16},{16,18},{18... | collective-permute-start | bytes 196616 | tf_op jit(solution)/shard_map/while/body/ppermute | solution.py:14
  158.2 6.2 %collective-permute-start.1 = (f32[32,1,512]{2,1,0:T(1,128)S(1)}, f32[32,1,512]{2,1,0:T(1,128)S(1)}, u32[]{:S(2)}, u32[]{:S(2)}) collective-permute-start(f32[32,1,512]{2,1,0:T(1,128)S(1)} %get-tuple-element.150), channel_id=1, source_target_pairs={{0,2},{2,4},{4,6},{6,8},{8,10},{10,12},{12,14},{14,16},{16,18},{18... | collective-permute-start | bytes 196616 | tf_op jit(solution)/shard_map/while/body/ppermute | solution.py:14
  172.3 6.2 %collective-permute-start.1 = (f32[32,1,512]{2,1,0:T(1,128)S(1)}, f32[32,1,512]{2,1,0:T(1,128)S(1)}, u32[]{:S(2)}, u32[]{:S(2)}) collective-permute-start(f32[32,1,512]{2,1,0:T(1,128)S(1)} %get-tuple-element.150), channel_id=1, source_target_pairs={{0,2},{2,4},{4,6},{6,8},{8,10},{10,12},{12,14},{14,16},{16,18},{18... | collective-permute-start | bytes 196616 | tf_op jit(solution)/shard_map/while/body/ppermute | solution.py:14
  186.4 6.2 %collective-permute-start.1 = (f32[32,1,512]{2,1,0:T(1,128)S(1)}, f32[32,1,512]{2,1,0:T(1,128)S(1)}, u32[]{:S(2)}, u32[]{:S(2)}) collective-permute-start(f32[32,1,512]{2,1,0:T(1,128)S(1)} %get-tuple-element.150), channel_id=1, source_target_pairs={{0,2},{2,4},{4,6},{6,8},{8,10},{10,12},{12,14},{14,16},{16,18},{18... | collective-permute-start | bytes 196616 | tf_op jit(solution)/shard_map/while/body/ppermute | solution.py:14
  200.6 6.2 %collective-permute-start.1 = (f32[32,1,512]{2,1,0:T(1,128)S(1)}, f32[32,1,512]{2,1,0:T(1,128)S(1)}, u32[]{:S(2)}, u32[]{:S(2)}) collective-permute-start(f32[32,1,512]{2,1,0:T(1,128)S(1)} %get-tuple-element.150), channel_id=1, source_target_pairs={{0,2},{2,4},{4,6},{6,8},{8,10},{10,12},{12,14},{14,16},{16,18},{18... | collective-permute-start | bytes 196616 | tf_op jit(solution)/shard_map/while/body/ppermute | solution.py:14
  214.7 6.2 %collective-permute-start.1 = (f32[32,1,512]{2,1,0:T(1,128)S(1)}, f32[32,1,512]{2,1,0:T(1,128)S(1)}, u32[]{:S(2)}, u32[]{:S(2)}) collective-permute-start(f32[32,1,512]{2,1,0:T(1,128)S(1)} %get-tuple-element.150), channel_id=1, source_target_pairs={{0,2},{2,4},{4,6},{6,8},{8,10},{10,12},{12,14},{14,16},{16,18},{18... | collective-permute-start | bytes 196616 | tf_op jit(solution)/shard_map/while/body/ppermute | solution.py:14
  228.8 6.2 %collective-permute-start.1 = (f32[32,1,512]{2,1,0:T(1,128)S(1)}, f32[32,1,512]{2,1,0:T(1,128)S(1)}, u32[]{:S(2)}, u32[]{:S(2)}) collective-permute-start(f32[32,1,512]{2,1,0:T(1,128)S(1)} %get-tuple-element.150), channel_id=1, source_target_pairs={{0,2},{2,4},{4,6},{6,8},{8,10},{10,12},{12,14},{14,16},{16,18},{18... | collective-permute-start | bytes 196616 | tf_op jit(solution)/shard_map/while/body/ppermute | solution.py:14
  243.0 6.2 %collective-permute-start.1 = (f32[32,1,512]{2,1,0:T(1,128)S(1)}, f32[32,1,512]{2,1,0:T(1,128)S(1)}, u32[]{:S(2)}, u32[]{:S(2)}) collective-permute-start(f32[32,1,512]{2,1,0:T(1,128)S(1)} %get-tuple-element.150), channel_id=1, source_target_pairs={{0,2},{2,4},{4,6},{6,8},{8,10},{10,12},{12,14},{14,16},{16,18},{18... | collective-permute-start | bytes 196616 | tf_op jit(solution)/shard_map/while/body/ppermute | solution.py:14
  257.1 6.2 %collective-permute-start.1 = (f32[32,1,512]{2,1,0:T(1,128)S(1)}, f32[32,1,512]{2,1,0:T(1,128)S(1)}, u32[]{:S(2)}, u32[]{:S(2)}) collective-permute-start(f32[32,1,512]{2,1,0:T(1,128)S(1)} %get-tuple-element.150), channel_id=1, source_target_pairs={{0,2},{2,4},{4,6},{6,8},{8,10},{10,12},{12,14},{14,16},{16,18},{18... | collective-permute-start | bytes 196616 | tf_op jit(solution)/shard_map/while/body/ppermute | solution.py:14
  271.2 6.2 %collective-permute-start.1 = (f32[32,1,512]{2,1,0:T(1,128)S(1)}, f32[32,1,512]{2,1,0:T(1,128)S(1)}, u32[]{:S(2)}, u32[]{:S(2)}) collective-permute-start(f32[32,1,512]{2,1,0:T(1,128)S(1)} %get-tuple-element.150), channel_id=1, source_target_pairs={{0,2},{2,4},{4,6},{6,8},{8,10},{10,12},{12,14},{14,16},{16,18},{18... | collective-permute-start | bytes 196616 | tf_op jit(solution)/shard_map/while/body/ppermute | solution.py:14
  285.4 6.2 %collective-permute-start.1 = (f32[32,1,512]{2,1,0:T(1,128)S(1)}, f32[32,1,512]{2,1,0:T(1,128)S(1)}, u32[]{:S(2)}, u32[]{:S(2)}) collective-permute-start(f32[32,1,512]{2,1,0:T(1,128)S(1)} %get-tuple-element.150), channel_id=1, source_target_pairs={{0,2},{2,4},{4,6},{6,8},{8,10},{10,12},{12,14},{14,16},{16,18},{18... | collective-permute-start | bytes 196616 | tf_op jit(solution)/shard_map/while/body/ppermute | solution.py:14
  299.5 6.2 %collective-permute-start.1 = (f32[32,1,512]{2,1,0:T(1,128)S(1)}, f32[32,1,512]{2,1,0:T(1,128)S(1)}, u32[]{:S(2)}, u32[]{:S(2)}) collective-permute-start(f32[32,1,512]{2,1,0:T(1,128)S(1)} %get-tuple-element.150), channel_id=1, source_target_pairs={{0,2},{2,4},{4,6},{6,8},{8,10},{10,12},{12,14},{14,16},{16,18},{18... | collective-permute-start | bytes 196616 | tf_op jit(solution)/shard_map/while/body/ppermute | solution.py:14
  313.6 6.2 %collective-permute-start.1 = (f32[32,1,512]{2,1,0:T(1,128)S(1)}, f32[32,1,512]{2,1,0:T(1,128)S(1)}, u32[]{:S(2)}, u32[]{:S(2)}) collective-permute-start(f32[32,1,512]{2,1,0:T(1,128)S(1)} %get-tuple-element.150), channel_id=1, source_target_pairs={{0,2},{2,4},{4,6},{6,8},{8,10},{10,12},{12,14},{14,16},{16,18},{18... | collective-permute-start | bytes 196616 | tf_op jit(solution)/shard_map/while/body/ppermute | solution.py:14
  327.8 6.2 %collective-permute-start.1 = (f32[32,1,512]{2,1,0:T(1,128)S(1)}, f32[32,1,512]{2,1,0:T(1,128)S(1)}, u32[]{:S(2)}, u32[]{:S(2)}) collective-permute-start(f32[32,1,512]{2,1,0:T(1,128)S(1)} %get-tuple-element.150), channel_id=1, source_target_pairs={{0,2},{2,4},{4,6},{6,8},{8,10},{10,12},{12,14},{14,16},{16,18},{18... | collective-permute-start | bytes 196616 | tf_op jit(solution)/shard_map/while/body/ppermute | solution.py:14
  341.9 6.2 %collective-permute-start.1 = (f32[32,1,512]{2,1,0:T(1,128)S(1)}, f32[32,1,512]{2,1,0:T(1,128)S(1)}, u32[]{:S(2)}, u32[]{:S(2)}) collective-permute-start(f32[32,1,512]{2,1,0:T(1,128)S(1)} %get-tuple-element.150), channel_id=1, source_target_pairs={{0,2},{2,4},{4,6},{6,8},{8,10},{10,12},{12,14},{14,16},{16,18},{18... | collective-permute-start | bytes 196616 | tf_op jit(solution)/shard_map/while/body/ppermute | solution.py:14
  356.1 6.2 %collective-permute-start.1 = (f32[32,1,512]{2,1,0:T(1,128)S(1)}, f32[32,1,512]{2,1,0:T(1,128)S(1)}, u32[]{:S(2)}, u32[]{:S(2)}) collective-permute-start(f32[32,1,512]{2,1,0:T(1,128)S(1)} %get-tuple-element.150), channel_id=1, source_target_pairs={{0,2},{2,4},{4,6},{6,8},{8,10},{10,12},{12,14},{14,16},{16,18},{18... | collective-permute-start | bytes 196616 | tf_op jit(solution)/shard_map/while/body/ppermute | solution.py:14
  370.2 6.2 %collective-permute-start.1 = (f32[32,1,512]{2,1,0:T(1,128)S(1)}, f32[32,1,512]{2,1,0:T(1,128)S(1)}, u32[]{:S(2)}, u32[]{:S(2)}) collective-permute-start(f32[32,1,512]{2,1,0:T(1,128)S(1)} %get-tuple-element.150), channel_id=1, source_target_pairs={{0,2},{2,4},{4,6},{6,8},{8,10},{10,12},{12,14},{14,16},{16,18},{18... | collective-permute-start | bytes 196616 | tf_op jit(solution)/shard_map/while/body/ppermute | solution.py:14
  384.3 6.2 %collective-permute-start.1 = (f32[32,1,512]{2,1,0:T(1,128)S(1)}, f32[32,1,512]{2,1,0:T(1,128)S(1)}, u32[]{:S(2)}, u32[]{:S(2)}) collective-permute-start(f32[32,1,512]{2,1,0:T(1,128)S(1)} %get-tuple-element.150), channel_id=1, source_target_pairs={{0,2},{2,4},{4,6},{6,8},{8,10},{10,12},{12,14},{14,16},{16,18},{18... | collective-permute-start | bytes 196616 | tf_op jit(solution)/shard_map/while/body/ppermute | solution.py:14
  398.5 6.2 %collective-permute-start.1 = (f32[32,1,512]{2,1,0:T(1,128)S(1)}, f32[32,1,512]{2,1,0:T(1,128)S(1)}, u32[]{:S(2)}, u32[]{:S(2)}) collective-permute-start(f32[32,1,512]{2,1,0:T(1,128)S(1)} %get-tuple-element.150), channel_id=1, source_target_pairs={{0,2},{2,4},{4,6},{6,8},{8,10},{10,12},{12,14},{14,16},{16,18},{18... | collective-permute-start | bytes 196616 | tf_op jit(solution)/shard_map/while/body/ppermute | solution.py:14
  412.6 6.2 %collective-permute-start.1 = (f32[32,1,512]{2,1,0:T(1,128)S(1)}, f32[32,1,512]{2,1,0:T(1,128)S(1)}, u32[]{:S(2)}, u32[]{:S(2)}) collective-permute-start(f32[32,1,512]{2,1,0:T(1,128)S(1)} %get-tuple-element.150), channel_id=1, source_target_pairs={{0,2},{2,4},{4,6},{6,8},{8,10},{10,12},{12,14},{14,16},{16,18},{18... | collective-permute-start | bytes 196616 | tf_op jit(solution)/shard_map/while/body/ppermute | solution.py:14
  426.7 6.2 %collective-permute-start.1 = (f32[32,1,512]{2,1,0:T(1,128)S(1)}, f32[32,1,512]{2,1,0:T(1,128)S(1)}, u32[]{:S(2)}, u32[]{:S(2)}) collective-permute-start(f32[32,1,512]{2,1,0:T(1,128)S(1)} %get-tuple-element.150), channel_id=1, source_target_pairs={{0,2},{2,4},{4,6},{6,8},{8,10},{10,12},{12,14},{14,16},{16,18},{18... | collective-permute-start | bytes 196616 | tf_op jit(solution)/shard_map/while/body/ppermute | solution.py:14
  440.9 6.2 %collective-permute-start.1 = (f32[32,1,512]{2,1,0:T(1,128)S(1)}, f32[32,1,512]{2,1,0:T(1,128)S(1)}, u32[]{:S(2)}, u32[]{:S(2)}) collective-permute-start(f32[32,1,512]{2,1,0:T(1,128)S(1)} %get-tuple-element.150), channel_id=1, source_target_pairs={{0,2},{2,4},{4,6},{6,8},{8,10},{10,12},{12,14},{14,16},{16,18},{18... | collective-permute-start | bytes 196616 | tf_op jit(solution)/shard_map/while/body/ppermute | solution.py:14
  455.0 6.2 %collective-permute-start.1 = (f32[32,1,512]{2,1,0:T(1,128)S(1)}, f32[32,1,512]{2,1,0:T(1,128)S(1)}, u32[]{:S(2)}, u32[]{:S(2)}) collective-permute-start(f32[32,1,512]{2,1,0:T(1,128)S(1)} %get-tuple-element.150), channel_id=1, source_target_pairs={{0,2},{2,4},{4,6},{6,8},{8,10},{10,12},{12,14},{14,16},{16,18},{18... | collective-permute-start | bytes 196616 | tf_op jit(solution)/shard_map/while/body/ppermute | solution.py:14
  481.4 50.6 %all-reduce.2 = (f32[64,64]{1,0:T(8,128)S(1)}, f32[64,64]{1,0:T(8,128)S(1)}) all-reduce(f32[64,64]{1,0:T(8,128)S(1)} %fusion.32, f32[64,64]{1,0:T(8,128)S(1)} %fusion.31), channel_id=1, replica_groups=mesh['space'=16,'ens'=2] {'space','ens'}, use_global_device_ids=true, to_apply=%region_7.8 | all-reduce | flops 8192 | bytes 65536 | tf_op jit(solution)/shard_map/psum | solution.py:83
  532.1 5.8 %cholesky.17 = f32[64,64]{1,0:T(8,128)S(1)} custom-call(f32[64,64]{1,0:T(8,128)S(1)} %fusion.23), custom_call_target="Cholesky" | custom-call | tf_op jit(solution)/shard_map/jit(cholesky)/cholesky | solution.py:51
  (319 shorter events, 290.8 us)
Async XLA Ops:
  7.2 537.7 %all-gather.2.cloned.1.call-start = ((), (), s32[]{:S(2)}) async-start(), calls=%async_computation.1 | async-start | bytes 3145728 | tf_op jit(solution)/shard_map/all_gather | solution.py:86
  47.8 7.4 %collective-permute-start = (f32[32,1,512]{2,1,0:T(1,128)S(1)}, f32[32,1,512]{2,1,0:T(1,128)S(1)}, u32[]{:S(2)}, u32[]{:S(2)}) collective-permute-start(f32[32,1,512]{2,1,0:T(1,128)S(1)} %get-tuple-element.149), channel_id=1, source_target_pairs={{2,0},{4,2},{6,4},{8,6},{10,8},{12,10},{14,12},{16,14},{18,16},{20... | collective-permute-start | bytes 196616 | tf_op jit(solution)/shard_map/while/body/ppermute | solution.py:17
  75.1 7.4 %collective-permute-start = (f32[32,1,512]{2,1,0:T(1,128)S(1)}, f32[32,1,512]{2,1,0:T(1,128)S(1)}, u32[]{:S(2)}, u32[]{:S(2)}) collective-permute-start(f32[32,1,512]{2,1,0:T(1,128)S(1)} %get-tuple-element.149), channel_id=1, source_target_pairs={{2,0},{4,2},{6,4},{8,6},{10,8},{12,10},{14,12},{16,14},{18,16},{20... | collective-permute-start | bytes 196616 | tf_op jit(solution)/shard_map/while/body/ppermute | solution.py:17
  89.0 7.4 %collective-permute-start = (f32[32,1,512]{2,1,0:T(1,128)S(1)}, f32[32,1,512]{2,1,0:T(1,128)S(1)}, u32[]{:S(2)}, u32[]{:S(2)}) collective-permute-start(f32[32,1,512]{2,1,0:T(1,128)S(1)} %get-tuple-element.149), channel_id=1, source_target_pairs={{2,0},{4,2},{6,4},{8,6},{10,8},{12,10},{14,12},{16,14},{18,16},{20... | collective-permute-start | bytes 196616 | tf_op jit(solution)/shard_map/while/body/ppermute | solution.py:17
  142.7 7.5 %collective-permute-start = (f32[32,1,512]{2,1,0:T(1,128)S(1)}, f32[32,1,512]{2,1,0:T(1,128)S(1)}, u32[]{:S(2)}, u32[]{:S(2)}) collective-permute-start(f32[32,1,512]{2,1,0:T(1,128)S(1)} %get-tuple-element.149), channel_id=1, source_target_pairs={{2,0},{4,2},{6,4},{8,6},{10,8},{12,10},{14,12},{16,14},{18,16},{20... | collective-permute-start | bytes 196616 | tf_op jit(solution)/shard_map/while/body/ppermute | solution.py:17
  156.9 7.5 %collective-permute-start = (f32[32,1,512]{2,1,0:T(1,128)S(1)}, f32[32,1,512]{2,1,0:T(1,128)S(1)}, u32[]{:S(2)}, u32[]{:S(2)}) collective-permute-start(f32[32,1,512]{2,1,0:T(1,128)S(1)} %get-tuple-element.149), channel_id=1, source_target_pairs={{2,0},{4,2},{6,4},{8,6},{10,8},{12,10},{14,12},{16,14},{18,16},{20... | collective-permute-start | bytes 196616 | tf_op jit(solution)/shard_map/while/body/ppermute | solution.py:17
  158.2 7.1 %collective-permute-start.1 = (f32[32,1,512]{2,1,0:T(1,128)S(1)}, f32[32,1,512]{2,1,0:T(1,128)S(1)}, u32[]{:S(2)}, u32[]{:S(2)}) collective-permute-start(f32[32,1,512]{2,1,0:T(1,128)S(1)} %get-tuple-element.150), channel_id=1, source_target_pairs={{0,2},{2,4},{4,6},{6,8},{8,10},{10,12},{12,14},{14,16},{16,18},{18... | collective-permute-start | bytes 196616 | tf_op jit(solution)/shard_map/while/body/ppermute | solution.py:14
  171.0 7.5 %collective-permute-start = (f32[32,1,512]{2,1,0:T(1,128)S(1)}, f32[32,1,512]{2,1,0:T(1,128)S(1)}, u32[]{:S(2)}, u32[]{:S(2)}) collective-permute-start(f32[32,1,512]{2,1,0:T(1,128)S(1)} %get-tuple-element.149), channel_id=1, source_target_pairs={{2,0},{4,2},{6,4},{8,6},{10,8},{12,10},{14,12},{16,14},{18,16},{20... | collective-permute-start | bytes 196616 | tf_op jit(solution)/shard_map/while/body/ppermute | solution.py:17
  185.1 7.5 %collective-permute-start = (f32[32,1,512]{2,1,0:T(1,128)S(1)}, f32[32,1,512]{2,1,0:T(1,128)S(1)}, u32[]{:S(2)}, u32[]{:S(2)}) collective-permute-start(f32[32,1,512]{2,1,0:T(1,128)S(1)} %get-tuple-element.149), channel_id=1, source_target_pairs={{2,0},{4,2},{6,4},{8,6},{10,8},{12,10},{14,12},{16,14},{18,16},{20... | collective-permute-start | bytes 196616 | tf_op jit(solution)/shard_map/while/body/ppermute | solution.py:17
  186.4 7.1 %collective-permute-start.1 = (f32[32,1,512]{2,1,0:T(1,128)S(1)}, f32[32,1,512]{2,1,0:T(1,128)S(1)}, u32[]{:S(2)}, u32[]{:S(2)}) collective-permute-start(f32[32,1,512]{2,1,0:T(1,128)S(1)} %get-tuple-element.150), channel_id=1, source_target_pairs={{0,2},{2,4},{4,6},{6,8},{8,10},{10,12},{12,14},{14,16},{16,18},{18... | collective-permute-start | bytes 196616 | tf_op jit(solution)/shard_map/while/body/ppermute | solution.py:14
  199.3 7.5 %collective-permute-start = (f32[32,1,512]{2,1,0:T(1,128)S(1)}, f32[32,1,512]{2,1,0:T(1,128)S(1)}, u32[]{:S(2)}, u32[]{:S(2)}) collective-permute-start(f32[32,1,512]{2,1,0:T(1,128)S(1)} %get-tuple-element.149), channel_id=1, source_target_pairs={{2,0},{4,2},{6,4},{8,6},{10,8},{12,10},{14,12},{16,14},{18,16},{20... | collective-permute-start | bytes 196616 | tf_op jit(solution)/shard_map/while/body/ppermute | solution.py:17
  200.6 7.1 %collective-permute-start.1 = (f32[32,1,512]{2,1,0:T(1,128)S(1)}, f32[32,1,512]{2,1,0:T(1,128)S(1)}, u32[]{:S(2)}, u32[]{:S(2)}) collective-permute-start(f32[32,1,512]{2,1,0:T(1,128)S(1)} %get-tuple-element.150), channel_id=1, source_target_pairs={{0,2},{2,4},{4,6},{6,8},{8,10},{10,12},{12,14},{14,16},{16,18},{18... | collective-permute-start | bytes 196616 | tf_op jit(solution)/shard_map/while/body/ppermute | solution.py:14
  213.4 7.5 %collective-permute-start = (f32[32,1,512]{2,1,0:T(1,128)S(1)}, f32[32,1,512]{2,1,0:T(1,128)S(1)}, u32[]{:S(2)}, u32[]{:S(2)}) collective-permute-start(f32[32,1,512]{2,1,0:T(1,128)S(1)} %get-tuple-element.149), channel_id=1, source_target_pairs={{2,0},{4,2},{6,4},{8,6},{10,8},{12,10},{14,12},{16,14},{18,16},{20... | collective-permute-start | bytes 196616 | tf_op jit(solution)/shard_map/while/body/ppermute | solution.py:17
  214.7 7.1 %collective-permute-start.1 = (f32[32,1,512]{2,1,0:T(1,128)S(1)}, f32[32,1,512]{2,1,0:T(1,128)S(1)}, u32[]{:S(2)}, u32[]{:S(2)}) collective-permute-start(f32[32,1,512]{2,1,0:T(1,128)S(1)} %get-tuple-element.150), channel_id=1, source_target_pairs={{0,2},{2,4},{4,6},{6,8},{8,10},{10,12},{12,14},{14,16},{16,18},{18... | collective-permute-start | bytes 196616 | tf_op jit(solution)/shard_map/while/body/ppermute | solution.py:14
  227.5 7.5 %collective-permute-start = (f32[32,1,512]{2,1,0:T(1,128)S(1)}, f32[32,1,512]{2,1,0:T(1,128)S(1)}, u32[]{:S(2)}, u32[]{:S(2)}) collective-permute-start(f32[32,1,512]{2,1,0:T(1,128)S(1)} %get-tuple-element.149), channel_id=1, source_target_pairs={{2,0},{4,2},{6,4},{8,6},{10,8},{12,10},{14,12},{16,14},{18,16},{20... | collective-permute-start | bytes 196616 | tf_op jit(solution)/shard_map/while/body/ppermute | solution.py:17
  241.7 7.5 %collective-permute-start = (f32[32,1,512]{2,1,0:T(1,128)S(1)}, f32[32,1,512]{2,1,0:T(1,128)S(1)}, u32[]{:S(2)}, u32[]{:S(2)}) collective-permute-start(f32[32,1,512]{2,1,0:T(1,128)S(1)} %get-tuple-element.149), channel_id=1, source_target_pairs={{2,0},{4,2},{6,4},{8,6},{10,8},{12,10},{14,12},{16,14},{18,16},{20... | collective-permute-start | bytes 196616 | tf_op jit(solution)/shard_map/while/body/ppermute | solution.py:17
  255.8 7.5 %collective-permute-start = (f32[32,1,512]{2,1,0:T(1,128)S(1)}, f32[32,1,512]{2,1,0:T(1,128)S(1)}, u32[]{:S(2)}, u32[]{:S(2)}) collective-permute-start(f32[32,1,512]{2,1,0:T(1,128)S(1)} %get-tuple-element.149), channel_id=1, source_target_pairs={{2,0},{4,2},{6,4},{8,6},{10,8},{12,10},{14,12},{16,14},{18,16},{20... | collective-permute-start | bytes 196616 | tf_op jit(solution)/shard_map/while/body/ppermute | solution.py:17
  269.9 7.5 %collective-permute-start = (f32[32,1,512]{2,1,0:T(1,128)S(1)}, f32[32,1,512]{2,1,0:T(1,128)S(1)}, u32[]{:S(2)}, u32[]{:S(2)}) collective-permute-start(f32[32,1,512]{2,1,0:T(1,128)S(1)} %get-tuple-element.149), channel_id=1, source_target_pairs={{2,0},{4,2},{6,4},{8,6},{10,8},{12,10},{14,12},{16,14},{18,16},{20... | collective-permute-start | bytes 196616 | tf_op jit(solution)/shard_map/while/body/ppermute | solution.py:17
  284.1 7.5 %collective-permute-start = (f32[32,1,512]{2,1,0:T(1,128)S(1)}, f32[32,1,512]{2,1,0:T(1,128)S(1)}, u32[]{:S(2)}, u32[]{:S(2)}) collective-permute-start(f32[32,1,512]{2,1,0:T(1,128)S(1)} %get-tuple-element.149), channel_id=1, source_target_pairs={{2,0},{4,2},{6,4},{8,6},{10,8},{12,10},{14,12},{16,14},{18,16},{20... | collective-permute-start | bytes 196616 | tf_op jit(solution)/shard_map/while/body/ppermute | solution.py:17
  298.2 7.5 %collective-permute-start = (f32[32,1,512]{2,1,0:T(1,128)S(1)}, f32[32,1,512]{2,1,0:T(1,128)S(1)}, u32[]{:S(2)}, u32[]{:S(2)}) collective-permute-start(f32[32,1,512]{2,1,0:T(1,128)S(1)} %get-tuple-element.149), channel_id=1, source_target_pairs={{2,0},{4,2},{6,4},{8,6},{10,8},{12,10},{14,12},{16,14},{18,16},{20... | collective-permute-start | bytes 196616 | tf_op jit(solution)/shard_map/while/body/ppermute | solution.py:17
  312.3 7.5 %collective-permute-start = (f32[32,1,512]{2,1,0:T(1,128)S(1)}, f32[32,1,512]{2,1,0:T(1,128)S(1)}, u32[]{:S(2)}, u32[]{:S(2)}) collective-permute-start(f32[32,1,512]{2,1,0:T(1,128)S(1)} %get-tuple-element.149), channel_id=1, source_target_pairs={{2,0},{4,2},{6,4},{8,6},{10,8},{12,10},{14,12},{16,14},{18,16},{20... | collective-permute-start | bytes 196616 | tf_op jit(solution)/shard_map/while/body/ppermute | solution.py:17
  326.5 7.5 %collective-permute-start = (f32[32,1,512]{2,1,0:T(1,128)S(1)}, f32[32,1,512]{2,1,0:T(1,128)S(1)}, u32[]{:S(2)}, u32[]{:S(2)}) collective-permute-start(f32[32,1,512]{2,1,0:T(1,128)S(1)} %get-tuple-element.149), channel_id=1, source_target_pairs={{2,0},{4,2},{6,4},{8,6},{10,8},{12,10},{14,12},{16,14},{18,16},{20... | collective-permute-start | bytes 196616 | tf_op jit(solution)/shard_map/while/body/ppermute | solution.py:17
  340.6 7.5 %collective-permute-start = (f32[32,1,512]{2,1,0:T(1,128)S(1)}, f32[32,1,512]{2,1,0:T(1,128)S(1)}, u32[]{:S(2)}, u32[]{:S(2)}) collective-permute-start(f32[32,1,512]{2,1,0:T(1,128)S(1)} %get-tuple-element.149), channel_id=1, source_target_pairs={{2,0},{4,2},{6,4},{8,6},{10,8},{12,10},{14,12},{16,14},{18,16},{20... | collective-permute-start | bytes 196616 | tf_op jit(solution)/shard_map/while/body/ppermute | solution.py:17
  354.8 7.5 %collective-permute-start = (f32[32,1,512]{2,1,0:T(1,128)S(1)}, f32[32,1,512]{2,1,0:T(1,128)S(1)}, u32[]{:S(2)}, u32[]{:S(2)}) collective-permute-start(f32[32,1,512]{2,1,0:T(1,128)S(1)} %get-tuple-element.149), channel_id=1, source_target_pairs={{2,0},{4,2},{6,4},{8,6},{10,8},{12,10},{14,12},{16,14},{18,16},{20... | collective-permute-start | bytes 196616 | tf_op jit(solution)/shard_map/while/body/ppermute | solution.py:17
  368.9 7.5 %collective-permute-start = (f32[32,1,512]{2,1,0:T(1,128)S(1)}, f32[32,1,512]{2,1,0:T(1,128)S(1)}, u32[]{:S(2)}, u32[]{:S(2)}) collective-permute-start(f32[32,1,512]{2,1,0:T(1,128)S(1)} %get-tuple-element.149), channel_id=1, source_target_pairs={{2,0},{4,2},{6,4},{8,6},{10,8},{12,10},{14,12},{16,14},{18,16},{20... | collective-permute-start | bytes 196616 | tf_op jit(solution)/shard_map/while/body/ppermute | solution.py:17
  383.0 7.5 %collective-permute-start = (f32[32,1,512]{2,1,0:T(1,128)S(1)}, f32[32,1,512]{2,1,0:T(1,128)S(1)}, u32[]{:S(2)}, u32[]{:S(2)}) collective-permute-start(f32[32,1,512]{2,1,0:T(1,128)S(1)} %get-tuple-element.149), channel_id=1, source_target_pairs={{2,0},{4,2},{6,4},{8,6},{10,8},{12,10},{14,12},{16,14},{18,16},{20... | collective-permute-start | bytes 196616 | tf_op jit(solution)/shard_map/while/body/ppermute | solution.py:17
  397.2 7.5 %collective-permute-start = (f32[32,1,512]{2,1,0:T(1,128)S(1)}, f32[32,1,512]{2,1,0:T(1,128)S(1)}, u32[]{:S(2)}, u32[]{:S(2)}) collective-permute-start(f32[32,1,512]{2,1,0:T(1,128)S(1)} %get-tuple-element.149), channel_id=1, source_target_pairs={{2,0},{4,2},{6,4},{8,6},{10,8},{12,10},{14,12},{16,14},{18,16},{20... | collective-permute-start | bytes 196616 | tf_op jit(solution)/shard_map/while/body/ppermute | solution.py:17
  411.3 7.5 %collective-permute-start = (f32[32,1,512]{2,1,0:T(1,128)S(1)}, f32[32,1,512]{2,1,0:T(1,128)S(1)}, u32[]{:S(2)}, u32[]{:S(2)}) collective-permute-start(f32[32,1,512]{2,1,0:T(1,128)S(1)} %get-tuple-element.149), channel_id=1, source_target_pairs={{2,0},{4,2},{6,4},{8,6},{10,8},{12,10},{14,12},{16,14},{18,16},{20... | collective-permute-start | bytes 196616 | tf_op jit(solution)/shard_map/while/body/ppermute | solution.py:17
  425.4 7.5 %collective-permute-start = (f32[32,1,512]{2,1,0:T(1,128)S(1)}, f32[32,1,512]{2,1,0:T(1,128)S(1)}, u32[]{:S(2)}, u32[]{:S(2)}) collective-permute-start(f32[32,1,512]{2,1,0:T(1,128)S(1)} %get-tuple-element.149), channel_id=1, source_target_pairs={{2,0},{4,2},{6,4},{8,6},{10,8},{12,10},{14,12},{16,14},{18,16},{20... | collective-permute-start | bytes 196616 | tf_op jit(solution)/shard_map/while/body/ppermute | solution.py:17
  439.6 7.5 %collective-permute-start = (f32[32,1,512]{2,1,0:T(1,128)S(1)}, f32[32,1,512]{2,1,0:T(1,128)S(1)}, u32[]{:S(2)}, u32[]{:S(2)}) collective-permute-start(f32[32,1,512]{2,1,0:T(1,128)S(1)} %get-tuple-element.149), channel_id=1, source_target_pairs={{2,0},{4,2},{6,4},{8,6},{10,8},{12,10},{14,12},{16,14},{18,16},{20... | collective-permute-start | bytes 196616 | tf_op jit(solution)/shard_map/while/body/ppermute | solution.py:17
  453.7 7.5 %collective-permute-start = (f32[32,1,512]{2,1,0:T(1,128)S(1)}, f32[32,1,512]{2,1,0:T(1,128)S(1)}, u32[]{:S(2)}, u32[]{:S(2)}) collective-permute-start(f32[32,1,512]{2,1,0:T(1,128)S(1)} %get-tuple-element.149), channel_id=1, source_target_pairs={{2,0},{4,2},{6,4},{8,6},{10,8},{12,10},{14,12},{16,14},{18,16},{20... | collective-permute-start | bytes 196616 | tf_op jit(solution)/shard_map/while/body/ppermute | solution.py:17
  473.7 7.2 %all-to-all-start = ((f32[32,2,128]{2,0,1:T(8,128)}), f32[32,2,128]{2,0,1:T(8,128)S(1)}, u32[]{:S(2)}, u32[]{:S(2)}) async-start(f32[32,2,128]{2,0,1:T(8,128)} %broadcast_select_fusion), calls=%async_computation | async-start | bytes 65536 | tf_op jit(solution)/shard_map/all_to_all | solution.py:78
  (44 other events, 298.3 us)
Sparse Core Ops, SparseCore 0:
  9.5 35.8 all-gather.1
where the time goes:
time: 566 us; the launch traced here: 561 us
  starting transfers between devices  242 us (43%)
  other arithmetic  136 us (24%)
  local copies, waits for them, and re-layouts  57.3 us (10%)
  blocking collectives  50.6 us (9%)
  waiting for transfers between devices  35.1 us (6%)
  loops' own time  21.8 us (4%)
  between operations  14.3 us (3%)
    ppermute x33, starting transfers between devices, padded_2(): lax.ppermute(lax.slice_in_dim(block, block.shape[dim] - width, None, axis...  196 us
    select_n x32, other arithmetic, advance(): return jnp.where((step_index < own_counts)[:, None, None], moved, thickness)  87.3 us
    psum x1, blocking collectives, shards(): gram, cross = lax.psum((gram, cross), ('space', 'ens'))  50.6 us
    ppermute x33, starting transfers between devices, padded_2(): lax.ppermute(lax.slice_in_dim(block, 0, width, axis=dim), axis, backward)  42.6 us
    while x32, local copies, waits for them, and re-layouts  39.3 us
    div x32, other arithmetic, stencil(): diffusivity = slip_padded * padded * padded / (1.0 + padded * padded)  32.8 us
    ppermute x33, waiting for transfers between devices, padded_2(): lax.ppermute(lax.slice_in_dim(block, block.shape[dim] - width, None, axis...  27.4 us
    another operation x1, loops' own time, shards(): thickness = lax.fori_loop(0, longest, advance, initial)  21.8 us
  transfers between devices with their start and end apart: 68, of which 34 were waited for; matrix products, arithmetic and copies ran while one was open for 34% of the time, Pallas kernels for 0%

commit v1 on v0

--- a/solution.py
+++ b/solution.py
@@ -80,7 +80,7 @@
     observed_part = lax.dynamic_slice_in_dim(observed, ens_index * block_width, block_width)
     noise_part = lax.dynamic_slice_in_dim(noise_var, ens_index * block_width, block_width)
     gram, cross = ensemble_terms(obs_block, observed_part, noise_part)
-    gram, cross = lax.psum((gram, cross), ("space", "ens"))
+    gram, cross = lax.psum(lax.psum((gram, cross), "ens"), "space")
     weights = solve_weights(gram, cross)
     weight_cols = lax.dynamic_slice_in_dim(weights, ens_index * members_dev, members_dev, 1)
     piece = lax.all_gather(params, "ens", axis=0, tiled=True)

time: 566 us -> 589 us (1.041)
  blocking collectives: 50.6 us -> 73.8 us
    psum x1 -> x2, blocking collectives: 50.6 us -> 73.8 us  [shards(): gram, cross = lax.psum(lax.psum((gram, cross), 'ens'), 'space')]
  transfers between devices with their start and end apart: 68 -> 68, of which waited for: 34 -> 34; matrix products, arithmetic and copies ran while one was open for 34% -> 32% of each run, Pallas kernels for 0% -> 0%
where the time goes in v1:
time: 589 us; the launch traced here: 585 us
  starting transfers between devices  242 us (41%)
  other arithmetic  136 us (23%)
  blocking collectives  73.8 us (13%)
  local copies, waits for them, and re-layouts  57.3 us (10%)
  waiting for transfers between devices  35.1 us (6%)
  loops' own time  22.7 us (4%)
  between operations  14.3 us (2%)
    ppermute x33, starting transfers between devices, padded_2(): lax.ppermute(lax.slice_in_dim(block, block.shape[dim] - width, None, axis...  196 us
    select_n x32, other arithmetic, advance(): return jnp.where((step_index < own_counts)[:, None, None], moved, thickness)  87.3 us
    psum x2, blocking collectives, shards(): gram, cross = lax.psum(lax.psum((gram, cross), 'ens'), 'space')  73.8 us
    ppermute x33, starting transfers between devices, padded_2(): lax.ppermute(lax.slice_in_dim(block, 0, width, axis=dim), axis, backward)  42.6 us
    while x32, local copies, waits for them, and re-layouts  39.3 us
    div x32, other arithmetic, stencil(): diffusivity = slip_padded * padded * padded / (1.0 + padded * padded)  32.8 us
    ppermute x33, waiting for transfers between devices, padded_2(): lax.ppermute(lax.slice_in_dim(block, block.shape[dim] - width, None, axis...  27.4 us
    another operation x1, loops' own time, shards(): thickness = lax.fori_loop(0, longest, advance, initial)  22.7 us
  transfers between devices with their start and end apart: 68, of which 34 were waited for; matrix products, arithmetic and copies ran while one was open for 32% of the time, Pallas kernels for 0%

profile of v1, /device:TPU:0, one launch (start us, length us, event | category | flops | bytes accessed | tf_op | source)
XLA Modules:
  0.0 584.9 jit_solution(14355301836889301861)
XLA Ops:
  19.3 448.1 %while.12 = (s32[]{:T(128)}, f32[32,16,512]{2,1,0:T(8,128)}, s32[]{:T(128)}, s32[32]{0:T(128)S(1)}, f32[32,18,514]{2,1,0:T(8,128)S(1)}, /*index=5*/f32[16,512]{1,0:T(8,128)S(1)}, s32[]{:T(128)}) while((s32[]{:T(128)}, f32[32,16,512]{2,1,0:T(8,128)}, s32[]{:T(128)}, s32[32]{0:T(128)S(1)}, f32[32,18,514]{2,1,0:T(8,128)S(1)}, ...), condition=%wide.region_2.3_spmd, body=%wide.region_1.2_spmd.sunk | while | flops 10402466 | bytes 17217376 | solution.py:75
  22.6 5.4 collective-permute-start.1
  49.2 6.0 %collective-permute-start.1 = (f32[32,1,512]{2,1,0:T(1,128)S(1)}, f32[32,1,512]{2,1,0:T(1,128)S(1)}, u32[]{:S(2)}, u32[]{:S(2)}) collective-permute-start(f32[32,1,512]{2,1,0:T(1,128)S(1)} %get-tuple-element.152), channel_id=1, source_target_pairs={{0,2},{2,4},{4,6},{6,8},{8,10},{10,12},{12,14},{14,16},{16,18},{18... | collective-permute-start | bytes 196616 | tf_op jit(solution)/shard_map/while/body/ppermute | solution.py:14
  63.2 5.4 collective-permute-start.1
  76.5 6.0 %collective-permute-start.1 = (f32[32,1,512]{2,1,0:T(1,128)S(1)}, f32[32,1,512]{2,1,0:T(1,128)S(1)}, u32[]{:S(2)}, u32[]{:S(2)}) collective-permute-start(f32[32,1,512]{2,1,0:T(1,128)S(1)} %get-tuple-element.152), channel_id=1, source_target_pairs={{0,2},{2,4},{4,6},{6,8},{8,10},{10,12},{12,14},{14,16},{16,18},{18... | collective-permute-start | bytes 196616 | tf_op jit(solution)/shard_map/while/body/ppermute | solution.py:14
  90.5 6.0 %collective-permute-start.1 = (f32[32,1,512]{2,1,0:T(1,128)S(1)}, f32[32,1,512]{2,1,0:T(1,128)S(1)}, u32[]{:S(2)}, u32[]{:S(2)}) collective-permute-start(f32[32,1,512]{2,1,0:T(1,128)S(1)} %get-tuple-element.152), channel_id=1, source_target_pairs={{0,2},{2,4},{4,6},{6,8},{8,10},{10,12},{12,14},{14,16},{16,18},{18... | collective-permute-start | bytes 196616 | tf_op jit(solution)/shard_map/while/body/ppermute | solution.py:14
  144.3 6.2 %collective-permute-start.1 = (f32[32,1,512]{2,1,0:T(1,128)S(1)}, f32[32,1,512]{2,1,0:T(1,128)S(1)}, u32[]{:S(2)}, u32[]{:S(2)}) collective-permute-start(f32[32,1,512]{2,1,0:T(1,128)S(1)} %get-tuple-element.152), channel_id=1, source_target_pairs={{0,2},{2,4},{4,6},{6,8},{8,10},{10,12},{12,14},{14,16},{16,18},{18... | collective-permute-start | bytes 196616 | tf_op jit(solution)/shard_map/while/body/ppermute | solution.py:14
  158.4 6.2 %collective-permute-start.1 = (f32[32,1,512]{2,1,0:T(1,128)S(1)}, f32[32,1,512]{2,1,0:T(1,128)S(1)}, u32[]{:S(2)}, u32[]{:S(2)}) collective-permute-start(f32[32,1,512]{2,1,0:T(1,128)S(1)} %get-tuple-element.152), channel_id=1, source_target_pairs={{0,2},{2,4},{4,6},{6,8},{8,10},{10,12},{12,14},{14,16},{16,18},{18... | collective-permute-start | bytes 196616 | tf_op jit(solution)/shard_map/while/body/ppermute | solution.py:14
  172.6 6.2 %collective-permute-start.1 = (f32[32,1,512]{2,1,0:T(1,128)S(1)}, f32[32,1,512]{2,1,0:T(1,128)S(1)}, u32[]{:S(2)}, u32[]{:S(2)}) collective-permute-start(f32[32,1,512]{2,1,0:T(1,128)S(1)} %get-tuple-element.152), channel_id=1, source_target_pairs={{0,2},{2,4},{4,6},{6,8},{8,10},{10,12},{12,14},{14,16},{16,18},{18... | collective-permute-start | bytes 196616 | tf_op jit(solution)/shard_map/while/body/ppermute | solution.py:14
  186.8 6.2 %collective-permute-start.1 = (f32[32,1,512]{2,1,0:T(1,128)S(1)}, f32[32,1,512]{2,1,0:T(1,128)S(1)}, u32[]{:S(2)}, u32[]{:S(2)}) collective-permute-start(f32[32,1,512]{2,1,0:T(1,128)S(1)} %get-tuple-element.152), channel_id=1, source_target_pairs={{0,2},{2,4},{4,6},{6,8},{8,10},{10,12},{12,14},{14,16},{16,18},{18... | collective-permute-start | bytes 196616 | tf_op jit(solution)/shard_map/while/body/ppermute | solution.py:14
  200.9 6.2 %collective-permute-start.1 = (f32[32,1,512]{2,1,0:T(1,128)S(1)}, f32[32,1,512]{2,1,0:T(1,128)S(1)}, u32[]{:S(2)}, u32[]{:S(2)}) collective-permute-start(f32[32,1,512]{2,1,0:T(1,128)S(1)} %get-tuple-element.152), channel_id=1, source_target_pairs={{0,2},{2,4},{4,6},{6,8},{8,10},{10,12},{12,14},{14,16},{16,18},{18... | collective-permute-start | bytes 196616 | tf_op jit(solution)/shard_map/while/body/ppermute | solution.py:14
  215.1 6.2 %collective-permute-start.1 = (f32[32,1,512]{2,1,0:T(1,128)S(1)}, f32[32,1,512]{2,1,0:T(1,128)S(1)}, u32[]{:S(2)}, u32[]{:S(2)}) collective-permute-start(f32[32,1,512]{2,1,0:T(1,128)S(1)} %get-tuple-element.152), channel_id=1, source_target_pairs={{0,2},{2,4},{4,6},{6,8},{8,10},{10,12},{12,14},{14,16},{16,18},{18... | collective-permute-start | bytes 196616 | tf_op jit(solution)/shard_map/while/body/ppermute | solution.py:14
  229.3 6.2 %collective-permute-start.1 = (f32[32,1,512]{2,1,0:T(1,128)S(1)}, f32[32,1,512]{2,1,0:T(1,128)S(1)}, u32[]{:S(2)}, u32[]{:S(2)}) collective-permute-start(f32[32,1,512]{2,1,0:T(1,128)S(1)} %get-tuple-element.152), channel_id=1, source_target_pairs={{0,2},{2,4},{4,6},{6,8},{8,10},{10,12},{12,14},{14,16},{16,18},{18... | collective-permute-start | bytes 196616 | tf_op jit(solution)/shard_map/while/body/ppermute | solution.py:14
  243.4 6.2 %collective-permute-start.1 = (f32[32,1,512]{2,1,0:T(1,128)S(1)}, f32[32,1,512]{2,1,0:T(1,128)S(1)}, u32[]{:S(2)}, u32[]{:S(2)}) collective-permute-start(f32[32,1,512]{2,1,0:T(1,128)S(1)} %get-tuple-element.152), channel_id=1, source_target_pairs={{0,2},{2,4},{4,6},{6,8},{8,10},{10,12},{12,14},{14,16},{16,18},{18... | collective-permute-start | bytes 196616 | tf_op jit(solution)/shard_map/while/body/ppermute | solution.py:14
  257.6 6.2 %collective-permute-start.1 = (f32[32,1,512]{2,1,0:T(1,128)S(1)}, f32[32,1,512]{2,1,0:T(1,128)S(1)}, u32[]{:S(2)}, u32[]{:S(2)}) collective-permute-start(f32[32,1,512]{2,1,0:T(1,128)S(1)} %get-tuple-element.152), channel_id=1, source_target_pairs={{0,2},{2,4},{4,6},{6,8},{8,10},{10,12},{12,14},{14,16},{16,18},{18... | collective-permute-start | bytes 196616 | tf_op jit(solution)/shard_map/while/body/ppermute | solution.py:14
  271.7 6.2 %collective-permute-start.1 = (f32[32,1,512]{2,1,0:T(1,128)S(1)}, f32[32,1,512]{2,1,0:T(1,128)S(1)}, u32[]{:S(2)}, u32[]{:S(2)}) collective-permute-start(f32[32,1,512]{2,1,0:T(1,128)S(1)} %get-tuple-element.152), channel_id=1, source_target_pairs={{0,2},{2,4},{4,6},{6,8},{8,10},{10,12},{12,14},{14,16},{16,18},{18... | collective-permute-start | bytes 196616 | tf_op jit(solution)/shard_map/while/body/ppermute | solution.py:14
  285.9 6.2 %collective-permute-start.1 = (f32[32,1,512]{2,1,0:T(1,128)S(1)}, f32[32,1,512]{2,1,0:T(1,128)S(1)}, u32[]{:S(2)}, u32[]{:S(2)}) collective-permute-start(f32[32,1,512]{2,1,0:T(1,128)S(1)} %get-tuple-element.152), channel_id=1, source_target_pairs={{0,2},{2,4},{4,6},{6,8},{8,10},{10,12},{12,14},{14,16},{16,18},{18... | collective-permute-start | bytes 196616 | tf_op jit(solution)/shard_map/while/body/ppermute | solution.py:14
  300.1 6.2 %collective-permute-start.1 = (f32[32,1,512]{2,1,0:T(1,128)S(1)}, f32[32,1,512]{2,1,0:T(1,128)S(1)}, u32[]{:S(2)}, u32[]{:S(2)}) collective-permute-start(f32[32,1,512]{2,1,0:T(1,128)S(1)} %get-tuple-element.152), channel_id=1, source_target_pairs={{0,2},{2,4},{4,6},{6,8},{8,10},{10,12},{12,14},{14,16},{16,18},{18... | collective-permute-start | bytes 196616 | tf_op jit(solution)/shard_map/while/body/ppermute | solution.py:14
  314.2 6.2 %collective-permute-start.1 = (f32[32,1,512]{2,1,0:T(1,128)S(1)}, f32[32,1,512]{2,1,0:T(1,128)S(1)}, u32[]{:S(2)}, u32[]{:S(2)}) collective-permute-start(f32[32,1,512]{2,1,0:T(1,128)S(1)} %get-tuple-element.152), channel_id=1, source_target_pairs={{0,2},{2,4},{4,6},{6,8},{8,10},{10,12},{12,14},{14,16},{16,18},{18... | collective-permute-start | bytes 196616 | tf_op jit(solution)/shard_map/while/body/ppermute | solution.py:14
  328.4 6.2 %collective-permute-start.1 = (f32[32,1,512]{2,1,0:T(1,128)S(1)}, f32[32,1,512]{2,1,0:T(1,128)S(1)}, u32[]{:S(2)}, u32[]{:S(2)}) collective-permute-start(f32[32,1,512]{2,1,0:T(1,128)S(1)} %get-tuple-element.152), channel_id=1, source_target_pairs={{0,2},{2,4},{4,6},{6,8},{8,10},{10,12},{12,14},{14,16},{16,18},{18... | collective-permute-start | bytes 196616 | tf_op jit(solution)/shard_map/while/body/ppermute | solution.py:14
  342.6 6.2 %collective-permute-start.1 = (f32[32,1,512]{2,1,0:T(1,128)S(1)}, f32[32,1,512]{2,1,0:T(1,128)S(1)}, u32[]{:S(2)}, u32[]{:S(2)}) collective-permute-start(f32[32,1,512]{2,1,0:T(1,128)S(1)} %get-tuple-element.152), channel_id=1, source_target_pairs={{0,2},{2,4},{4,6},{6,8},{8,10},{10,12},{12,14},{14,16},{16,18},{18... | collective-permute-start | bytes 196616 | tf_op jit(solution)/shard_map/while/body/ppermute | solution.py:14
  356.7 6.2 %collective-permute-start.1 = (f32[32,1,512]{2,1,0:T(1,128)S(1)}, f32[32,1,512]{2,1,0:T(1,128)S(1)}, u32[]{:S(2)}, u32[]{:S(2)}) collective-permute-start(f32[32,1,512]{2,1,0:T(1,128)S(1)} %get-tuple-element.152), channel_id=1, source_target_pairs={{0,2},{2,4},{4,6},{6,8},{8,10},{10,12},{12,14},{14,16},{16,18},{18... | collective-permute-start | bytes 196616 | tf_op jit(solution)/shard_map/while/body/ppermute | solution.py:14
  370.9 6.2 %collective-permute-start.1 = (f32[32,1,512]{2,1,0:T(1,128)S(1)}, f32[32,1,512]{2,1,0:T(1,128)S(1)}, u32[]{:S(2)}, u32[]{:S(2)}) collective-permute-start(f32[32,1,512]{2,1,0:T(1,128)S(1)} %get-tuple-element.152), channel_id=1, source_target_pairs={{0,2},{2,4},{4,6},{6,8},{8,10},{10,12},{12,14},{14,16},{16,18},{18... | collective-permute-start | bytes 196616 | tf_op jit(solution)/shard_map/while/body/ppermute | solution.py:14
  385.1 6.2 %collective-permute-start.1 = (f32[32,1,512]{2,1,0:T(1,128)S(1)}, f32[32,1,512]{2,1,0:T(1,128)S(1)}, u32[]{:S(2)}, u32[]{:S(2)}) collective-permute-start(f32[32,1,512]{2,1,0:T(1,128)S(1)} %get-tuple-element.152), channel_id=1, source_target_pairs={{0,2},{2,4},{4,6},{6,8},{8,10},{10,12},{12,14},{14,16},{16,18},{18... | collective-permute-start | bytes 196616 | tf_op jit(solution)/shard_map/while/body/ppermute | solution.py:14
  399.2 6.2 %collective-permute-start.1 = (f32[32,1,512]{2,1,0:T(1,128)S(1)}, f32[32,1,512]{2,1,0:T(1,128)S(1)}, u32[]{:S(2)}, u32[]{:S(2)}) collective-permute-start(f32[32,1,512]{2,1,0:T(1,128)S(1)} %get-tuple-element.152), channel_id=1, source_target_pairs={{0,2},{2,4},{4,6},{6,8},{8,10},{10,12},{12,14},{14,16},{16,18},{18... | collective-permute-start | bytes 196616 | tf_op jit(solution)/shard_map/while/body/ppermute | solution.py:14
  413.4 6.2 %collective-permute-start.1 = (f32[32,1,512]{2,1,0:T(1,128)S(1)}, f32[32,1,512]{2,1,0:T(1,128)S(1)}, u32[]{:S(2)}, u32[]{:S(2)}) collective-permute-start(f32[32,1,512]{2,1,0:T(1,128)S(1)} %get-tuple-element.152), channel_id=1, source_target_pairs={{0,2},{2,4},{4,6},{6,8},{8,10},{10,12},{12,14},{14,16},{16,18},{18... | collective-permute-start | bytes 196616 | tf_op jit(solution)/shard_map/while/body/ppermute | solution.py:14
  427.5 6.2 %collective-permute-start.1 = (f32[32,1,512]{2,1,0:T(1,128)S(1)}, f32[32,1,512]{2,1,0:T(1,128)S(1)}, u32[]{:S(2)}, u32[]{:S(2)}) collective-permute-start(f32[32,1,512]{2,1,0:T(1,128)S(1)} %get-tuple-element.152), channel_id=1, source_target_pairs={{0,2},{2,4},{4,6},{6,8},{8,10},{10,12},{12,14},{14,16},{16,18},{18... | collective-permute-start | bytes 196616 | tf_op jit(solution)/shard_map/while/body/ppermute | solution.py:14
  441.7 6.2 %collective-permute-start.1 = (f32[32,1,512]{2,1,0:T(1,128)S(1)}, f32[32,1,512]{2,1,0:T(1,128)S(1)}, u32[]{:S(2)}, u32[]{:S(2)}) collective-permute-start(f32[32,1,512]{2,1,0:T(1,128)S(1)} %get-tuple-element.152), channel_id=1, source_target_pairs={{0,2},{2,4},{4,6},{6,8},{8,10},{10,12},{12,14},{14,16},{16,18},{18... | collective-permute-start | bytes 196616 | tf_op jit(solution)/shard_map/while/body/ppermute | solution.py:14
  455.9 6.2 %collective-permute-start.1 = (f32[32,1,512]{2,1,0:T(1,128)S(1)}, f32[32,1,512]{2,1,0:T(1,128)S(1)}, u32[]{:S(2)}, u32[]{:S(2)}) collective-permute-start(f32[32,1,512]{2,1,0:T(1,128)S(1)} %get-tuple-element.152), channel_id=1, source_target_pairs={{0,2},{2,4},{4,6},{6,8},{8,10},{10,12},{12,14},{14,16},{16,18},{18... | collective-permute-start | bytes 196616 | tf_op jit(solution)/shard_map/while/body/ppermute | solution.py:14
  482.2 7.4 %all-reduce.3 = (f32[64,64]{1,0:T(8,128)S(1)}, f32[64,64]{1,0:T(8,128)S(1)}) all-reduce(f32[64,64]{1,0:T(8,128)S(1)} %fusion.32, f32[64,64]{1,0:T(8,128)S(1)} %fusion.31), channel_id=1, replica_groups=mesh['space'=16,'ens'=2] {'ens'}, use_global_device_ids=true, to_apply=%region_8.9 | all-reduce | flops 8192 | bytes 65536 | tf_op jit(solution)/shard_map/psum | solution.py:83
  489.6 66.5 %all-reduce.2 = (f32[64,64]{1,0:T(8,128)S(1)}, f32[64,64]{1,0:T(8,128)S(1)}) all-reduce(f32[64,64]{1,0:T(8,128)S(1)} %get-tuple-element.97, f32[64,64]{1,0:T(8,128)S(1)} %get-tuple-element.98), channel_id=1, replica_groups=mesh['space'=16,'ens'=2] {'space'}, use_global_device_ids=true, to_apply=%region_9.10 | all-reduce | flops 8192 | bytes 65536 | tf_op jit(solution)/shard_map/psum | solution.py:83
  556.2 5.8 cholesky.17
  (320 shorter events, 296.2 us)
Async XLA Ops:
  7.2 561.7 %all-gather.2.cloned.1.call-start = ((), (), s32[]{:S(2)}) async-start(), calls=%async_computation.1 | async-start | bytes 3145728 | tf_op jit(solution)/shard_map/all_gather | solution.py:86
  47.9 7.4 %collective-permute-start = (f32[32,1,512]{2,1,0:T(1,128)S(1)}, f32[32,1,512]{2,1,0:T(1,128)S(1)}, u32[]{:S(2)}, u32[]{:S(2)}) collective-permute-start(f32[32,1,512]{2,1,0:T(1,128)S(1)} %get-tuple-element.151), channel_id=1, source_target_pairs={{2,0},{4,2},{6,4},{8,6},{10,8},{12,10},{14,12},{16,14},{18,16},{20... | collective-permute-start | bytes 196616 | tf_op jit(solution)/shard_map/while/body/ppermute | solution.py:17
  75.2 7.4 %collective-permute-start = (f32[32,1,512]{2,1,0:T(1,128)S(1)}, f32[32,1,512]{2,1,0:T(1,128)S(1)}, u32[]{:S(2)}, u32[]{:S(2)}) collective-permute-start(f32[32,1,512]{2,1,0:T(1,128)S(1)} %get-tuple-element.151), channel_id=1, source_target_pairs={{2,0},{4,2},{6,4},{8,6},{10,8},{12,10},{14,12},{16,14},{18,16},{20... | collective-permute-start | bytes 196616 | tf_op jit(solution)/shard_map/while/body/ppermute | solution.py:17
  89.2 7.4 %collective-permute-start = (f32[32,1,512]{2,1,0:T(1,128)S(1)}, f32[32,1,512]{2,1,0:T(1,128)S(1)}, u32[]{:S(2)}, u32[]{:S(2)}) collective-permute-start(f32[32,1,512]{2,1,0:T(1,128)S(1)} %get-tuple-element.151), channel_id=1, source_target_pairs={{2,0},{4,2},{6,4},{8,6},{10,8},{12,10},{14,12},{16,14},{18,16},{20... | collective-permute-start | bytes 196616 | tf_op jit(solution)/shard_map/while/body/ppermute | solution.py:17
  143.0 7.5 %collective-permute-start = (f32[32,1,512]{2,1,0:T(1,128)S(1)}, f32[32,1,512]{2,1,0:T(1,128)S(1)}, u32[]{:S(2)}, u32[]{:S(2)}) collective-permute-start(f32[32,1,512]{2,1,0:T(1,128)S(1)} %get-tuple-element.151), channel_id=1, source_target_pairs={{2,0},{4,2},{6,4},{8,6},{10,8},{12,10},{14,12},{16,14},{18,16},{20... | collective-permute-start | bytes 196616 | tf_op jit(solution)/shard_map/while/body/ppermute | solution.py:17
  157.1 7.5 %collective-permute-start = (f32[32,1,512]{2,1,0:T(1,128)S(1)}, f32[32,1,512]{2,1,0:T(1,128)S(1)}, u32[]{:S(2)}, u32[]{:S(2)}) collective-permute-start(f32[32,1,512]{2,1,0:T(1,128)S(1)} %get-tuple-element.151), channel_id=1, source_target_pairs={{2,0},{4,2},{6,4},{8,6},{10,8},{12,10},{14,12},{16,14},{18,16},{20... | collective-permute-start | bytes 196616 | tf_op jit(solution)/shard_map/while/body/ppermute | solution.py:17
  158.4 7.1 %collective-permute-start.1 = (f32[32,1,512]{2,1,0:T(1,128)S(1)}, f32[32,1,512]{2,1,0:T(1,128)S(1)}, u32[]{:S(2)}, u32[]{:S(2)}) collective-permute-start(f32[32,1,512]{2,1,0:T(1,128)S(1)} %get-tuple-element.152), channel_id=1, source_target_pairs={{0,2},{2,4},{4,6},{6,8},{8,10},{10,12},{12,14},{14,16},{16,18},{18... | collective-permute-start | bytes 196616 | tf_op jit(solution)/shard_map/while/body/ppermute | solution.py:14
  171.3 7.5 %collective-permute-start = (f32[32,1,512]{2,1,0:T(1,128)S(1)}, f32[32,1,512]{2,1,0:T(1,128)S(1)}, u32[]{:S(2)}, u32[]{:S(2)}) collective-permute-start(f32[32,1,512]{2,1,0:T(1,128)S(1)} %get-tuple-element.151), channel_id=1, source_target_pairs={{2,0},{4,2},{6,4},{8,6},{10,8},{12,10},{14,12},{16,14},{18,16},{20... | collective-permute-start | bytes 196616 | tf_op jit(solution)/shard_map/while/body/ppermute | solution.py:17
  185.5 7.5 %collective-permute-start = (f32[32,1,512]{2,1,0:T(1,128)S(1)}, f32[32,1,512]{2,1,0:T(1,128)S(1)}, u32[]{:S(2)}, u32[]{:S(2)}) collective-permute-start(f32[32,1,512]{2,1,0:T(1,128)S(1)} %get-tuple-element.151), channel_id=1, source_target_pairs={{2,0},{4,2},{6,4},{8,6},{10,8},{12,10},{14,12},{16,14},{18,16},{20... | collective-permute-start | bytes 196616 | tf_op jit(solution)/shard_map/while/body/ppermute | solution.py:17
  186.8 7.1 %collective-permute-start.1 = (f32[32,1,512]{2,1,0:T(1,128)S(1)}, f32[32,1,512]{2,1,0:T(1,128)S(1)}, u32[]{:S(2)}, u32[]{:S(2)}) collective-permute-start(f32[32,1,512]{2,1,0:T(1,128)S(1)} %get-tuple-element.152), channel_id=1, source_target_pairs={{0,2},{2,4},{4,6},{6,8},{8,10},{10,12},{12,14},{14,16},{16,18},{18... | collective-permute-start | bytes 196616 | tf_op jit(solution)/shard_map/while/body/ppermute | solution.py:14
  199.6 7.5 %collective-permute-start = (f32[32,1,512]{2,1,0:T(1,128)S(1)}, f32[32,1,512]{2,1,0:T(1,128)S(1)}, u32[]{:S(2)}, u32[]{:S(2)}) collective-permute-start(f32[32,1,512]{2,1,0:T(1,128)S(1)} %get-tuple-element.151), channel_id=1, source_target_pairs={{2,0},{4,2},{6,4},{8,6},{10,8},{12,10},{14,12},{16,14},{18,16},{20... | collective-permute-start | bytes 196616 | tf_op jit(solution)/shard_map/while/body/ppermute | solution.py:17
  200.9 7.1 %collective-permute-start.1 = (f32[32,1,512]{2,1,0:T(1,128)S(1)}, f32[32,1,512]{2,1,0:T(1,128)S(1)}, u32[]{:S(2)}, u32[]{:S(2)}) collective-permute-start(f32[32,1,512]{2,1,0:T(1,128)S(1)} %get-tuple-element.152), channel_id=1, source_target_pairs={{0,2},{2,4},{4,6},{6,8},{8,10},{10,12},{12,14},{14,16},{16,18},{18... | collective-permute-start | bytes 196616 | tf_op jit(solution)/shard_map/while/body/ppermute | solution.py:14
  213.8 7.5 %collective-permute-start = (f32[32,1,512]{2,1,0:T(1,128)S(1)}, f32[32,1,512]{2,1,0:T(1,128)S(1)}, u32[]{:S(2)}, u32[]{:S(2)}) collective-permute-start(f32[32,1,512]{2,1,0:T(1,128)S(1)} %get-tuple-element.151), channel_id=1, source_target_pairs={{2,0},{4,2},{6,4},{8,6},{10,8},{12,10},{14,12},{16,14},{18,16},{20... | collective-permute-start | bytes 196616 | tf_op jit(solution)/shard_map/while/body/ppermute | solution.py:17
  228.0 7.5 %collective-permute-start = (f32[32,1,512]{2,1,0:T(1,128)S(1)}, f32[32,1,512]{2,1,0:T(1,128)S(1)}, u32[]{:S(2)}, u32[]{:S(2)}) collective-permute-start(f32[32,1,512]{2,1,0:T(1,128)S(1)} %get-tuple-element.151), channel_id=1, source_target_pairs={{2,0},{4,2},{6,4},{8,6},{10,8},{12,10},{14,12},{16,14},{18,16},{20... | collective-permute-start | bytes 196616 | tf_op jit(solution)/shard_map/while/body/ppermute | solution.py:17
  229.3 7.1 %collective-permute-start.1 = (f32[32,1,512]{2,1,0:T(1,128)S(1)}, f32[32,1,512]{2,1,0:T(1,128)S(1)}, u32[]{:S(2)}, u32[]{:S(2)}) collective-permute-start(f32[32,1,512]{2,1,0:T(1,128)S(1)} %get-tuple-element.152), channel_id=1, source_target_pairs={{0,2},{2,4},{4,6},{6,8},{8,10},{10,12},{12,14},{14,16},{16,18},{18... | collective-permute-start | bytes 196616 | tf_op jit(solution)/shard_map/while/body/ppermute | solution.py:14
  242.1 7.5 %collective-permute-start = (f32[32,1,512]{2,1,0:T(1,128)S(1)}, f32[32,1,512]{2,1,0:T(1,128)S(1)}, u32[]{:S(2)}, u32[]{:S(2)}) collective-permute-start(f32[32,1,512]{2,1,0:T(1,128)S(1)} %get-tuple-element.151), channel_id=1, source_target_pairs={{2,0},{4,2},{6,4},{8,6},{10,8},{12,10},{14,12},{16,14},{18,16},{20... | collective-permute-start | bytes 196616 | tf_op jit(solution)/shard_map/while/body/ppermute | solution.py:17
  256.3 7.5 %collective-permute-start = (f32[32,1,512]{2,1,0:T(1,128)S(1)}, f32[32,1,512]{2,1,0:T(1,128)S(1)}, u32[]{:S(2)}, u32[]{:S(2)}) collective-permute-start(f32[32,1,512]{2,1,0:T(1,128)S(1)} %get-tuple-element.151), channel_id=1, source_target_pairs={{2,0},{4,2},{6,4},{8,6},{10,8},{12,10},{14,12},{16,14},{18,16},{20... | collective-permute-start | bytes 196616 | tf_op jit(solution)/shard_map/while/body/ppermute | solution.py:17
  270.4 7.5 %collective-permute-start = (f32[32,1,512]{2,1,0:T(1,128)S(1)}, f32[32,1,512]{2,1,0:T(1,128)S(1)}, u32[]{:S(2)}, u32[]{:S(2)}) collective-permute-start(f32[32,1,512]{2,1,0:T(1,128)S(1)} %get-tuple-element.151), channel_id=1, source_target_pairs={{2,0},{4,2},{6,4},{8,6},{10,8},{12,10},{14,12},{16,14},{18,16},{20... | collective-permute-start | bytes 196616 | tf_op jit(solution)/shard_map/while/body/ppermute | solution.py:17
  284.6 7.5 %collective-permute-start = (f32[32,1,512]{2,1,0:T(1,128)S(1)}, f32[32,1,512]{2,1,0:T(1,128)S(1)}, u32[]{:S(2)}, u32[]{:S(2)}) collective-permute-start(f32[32,1,512]{2,1,0:T(1,128)S(1)} %get-tuple-element.151), channel_id=1, source_target_pairs={{2,0},{4,2},{6,4},{8,6},{10,8},{12,10},{14,12},{16,14},{18,16},{20... | collective-permute-start | bytes 196616 | tf_op jit(solution)/shard_map/while/body/ppermute | solution.py:17
  298.8 7.5 %collective-permute-start = (f32[32,1,512]{2,1,0:T(1,128)S(1)}, f32[32,1,512]{2,1,0:T(1,128)S(1)}, u32[]{:S(2)}, u32[]{:S(2)}) collective-permute-start(f32[32,1,512]{2,1,0:T(1,128)S(1)} %get-tuple-element.151), channel_id=1, source_target_pairs={{2,0},{4,2},{6,4},{8,6},{10,8},{12,10},{14,12},{16,14},{18,16},{20... | collective-permute-start | bytes 196616 | tf_op jit(solution)/shard_map/while/body/ppermute | solution.py:17
  312.9 7.5 %collective-permute-start = (f32[32,1,512]{2,1,0:T(1,128)S(1)}, f32[32,1,512]{2,1,0:T(1,128)S(1)}, u32[]{:S(2)}, u32[]{:S(2)}) collective-permute-start(f32[32,1,512]{2,1,0:T(1,128)S(1)} %get-tuple-element.151), channel_id=1, source_target_pairs={{2,0},{4,2},{6,4},{8,6},{10,8},{12,10},{14,12},{16,14},{18,16},{20... | collective-permute-start | bytes 196616 | tf_op jit(solution)/shard_map/while/body/ppermute | solution.py:17
  327.1 7.5 %collective-permute-start = (f32[32,1,512]{2,1,0:T(1,128)S(1)}, f32[32,1,512]{2,1,0:T(1,128)S(1)}, u32[]{:S(2)}, u32[]{:S(2)}) collective-permute-start(f32[32,1,512]{2,1,0:T(1,128)S(1)} %get-tuple-element.151), channel_id=1, source_target_pairs={{2,0},{4,2},{6,4},{8,6},{10,8},{12,10},{14,12},{16,14},{18,16},{20... | collective-permute-start | bytes 196616 | tf_op jit(solution)/shard_map/while/body/ppermute | solution.py:17
  341.3 7.5 %collective-permute-start = (f32[32,1,512]{2,1,0:T(1,128)S(1)}, f32[32,1,512]{2,1,0:T(1,128)S(1)}, u32[]{:S(2)}, u32[]{:S(2)}) collective-permute-start(f32[32,1,512]{2,1,0:T(1,128)S(1)} %get-tuple-element.151), channel_id=1, source_target_pairs={{2,0},{4,2},{6,4},{8,6},{10,8},{12,10},{14,12},{16,14},{18,16},{20... | collective-permute-start | bytes 196616 | tf_op jit(solution)/shard_map/while/body/ppermute | solution.py:17
  355.4 7.5 %collective-permute-start = (f32[32,1,512]{2,1,0:T(1,128)S(1)}, f32[32,1,512]{2,1,0:T(1,128)S(1)}, u32[]{:S(2)}, u32[]{:S(2)}) collective-permute-start(f32[32,1,512]{2,1,0:T(1,128)S(1)} %get-tuple-element.151), channel_id=1, source_target_pairs={{2,0},{4,2},{6,4},{8,6},{10,8},{12,10},{14,12},{16,14},{18,16},{20... | collective-permute-start | bytes 196616 | tf_op jit(solution)/shard_map/while/body/ppermute | solution.py:17
  369.6 7.5 %collective-permute-start = (f32[32,1,512]{2,1,0:T(1,128)S(1)}, f32[32,1,512]{2,1,0:T(1,128)S(1)}, u32[]{:S(2)}, u32[]{:S(2)}) collective-permute-start(f32[32,1,512]{2,1,0:T(1,128)S(1)} %get-tuple-element.151), channel_id=1, source_target_pairs={{2,0},{4,2},{6,4},{8,6},{10,8},{12,10},{14,12},{16,14},{18,16},{20... | collective-permute-start | bytes 196616 | tf_op jit(solution)/shard_map/while/body/ppermute | solution.py:17
  383.8 7.5 %collective-permute-start = (f32[32,1,512]{2,1,0:T(1,128)S(1)}, f32[32,1,512]{2,1,0:T(1,128)S(1)}, u32[]{:S(2)}, u32[]{:S(2)}) collective-permute-start(f32[32,1,512]{2,1,0:T(1,128)S(1)} %get-tuple-element.151), channel_id=1, source_target_pairs={{2,0},{4,2},{6,4},{8,6},{10,8},{12,10},{14,12},{16,14},{18,16},{20... | collective-permute-start | bytes 196616 | tf_op jit(solution)/shard_map/while/body/ppermute | solution.py:17
  397.9 7.5 %collective-permute-start = (f32[32,1,512]{2,1,0:T(1,128)S(1)}, f32[32,1,512]{2,1,0:T(1,128)S(1)}, u32[]{:S(2)}, u32[]{:S(2)}) collective-permute-start(f32[32,1,512]{2,1,0:T(1,128)S(1)} %get-tuple-element.151), channel_id=1, source_target_pairs={{2,0},{4,2},{6,4},{8,6},{10,8},{12,10},{14,12},{16,14},{18,16},{20... | collective-permute-start | bytes 196616 | tf_op jit(solution)/shard_map/while/body/ppermute | solution.py:17
  412.1 7.5 %collective-permute-start = (f32[32,1,512]{2,1,0:T(1,128)S(1)}, f32[32,1,512]{2,1,0:T(1,128)S(1)}, u32[]{:S(2)}, u32[]{:S(2)}) collective-permute-start(f32[32,1,512]{2,1,0:T(1,128)S(1)} %get-tuple-element.151), channel_id=1, source_target_pairs={{2,0},{4,2},{6,4},{8,6},{10,8},{12,10},{14,12},{16,14},{18,16},{20... | collective-permute-start | bytes 196616 | tf_op jit(solution)/shard_map/while/body/ppermute | solution.py:17
  426.2 7.5 %collective-permute-start = (f32[32,1,512]{2,1,0:T(1,128)S(1)}, f32[32,1,512]{2,1,0:T(1,128)S(1)}, u32[]{:S(2)}, u32[]{:S(2)}) collective-permute-start(f32[32,1,512]{2,1,0:T(1,128)S(1)} %get-tuple-element.151), channel_id=1, source_target_pairs={{2,0},{4,2},{6,4},{8,6},{10,8},{12,10},{14,12},{16,14},{18,16},{20... | collective-permute-start | bytes 196616 | tf_op jit(solution)/shard_map/while/body/ppermute | solution.py:17
  440.4 7.5 %collective-permute-start = (f32[32,1,512]{2,1,0:T(1,128)S(1)}, f32[32,1,512]{2,1,0:T(1,128)S(1)}, u32[]{:S(2)}, u32[]{:S(2)}) collective-permute-start(f32[32,1,512]{2,1,0:T(1,128)S(1)} %get-tuple-element.151), channel_id=1, source_target_pairs={{2,0},{4,2},{6,4},{8,6},{10,8},{12,10},{14,12},{16,14},{18,16},{20... | collective-permute-start | bytes 196616 | tf_op jit(solution)/shard_map/while/body/ppermute | solution.py:17
  454.6 7.5 %collective-permute-start = (f32[32,1,512]{2,1,0:T(1,128)S(1)}, f32[32,1,512]{2,1,0:T(1,128)S(1)}, u32[]{:S(2)}, u32[]{:S(2)}) collective-permute-start(f32[32,1,512]{2,1,0:T(1,128)S(1)} %get-tuple-element.151), channel_id=1, source_target_pairs={{2,0},{4,2},{6,4},{8,6},{10,8},{12,10},{14,12},{16,14},{18,16},{20... | collective-permute-start | bytes 196616 | tf_op jit(solution)/shard_map/while/body/ppermute | solution.py:17
  474.6 7.2 %all-to-all-start = ((f32[32,2,128]{2,0,1:T(8,128)}), f32[32,2,128]{2,0,1:T(8,128)S(1)}, u32[]{:S(2)}, u32[]{:S(2)}) async-start(f32[32,2,128]{2,0,1:T(8,128)} %broadcast_select_fusion), calls=%async_computation | async-start | bytes 65536 | tf_op jit(solution)/shard_map/all_to_all | solution.py:78
  (44 other events, 298.3 us)
Sparse Core Ops, SparseCore 0:
  9.5 35.8 all-gather.1
